TPU v7x, 512 devices: a whole 4x4x16 slice. The times are simulated.
512 devices in a mesh: shard: 128 (over z, y, core), tensor: 4 (over x).
Axes of the slice: x: 4, y: 4, z: 16, core: 2. Of those that a mesh axis runs over, the one named last changes fastest.
Arguments:
- wo_grads: bfloat16 [4, 2, 8, 8, 512, 512], P('tensor', None, None, None, 'shard'), may hold values from -6 to 6
- wo_master: float32 [2, 8, 8, 512, 512], P(None, None, None, 'shard', 'tensor'), may hold values from -0.09375 to 0.09375
- left_stats: float32 [256, 512, 512], P('shard', 'tensor'), may hold values from -6 to 6
- right_stats: float32 [256, 512, 512], P('shard', 'tensor'), may hold values from -6 to 6
- left_roots: bfloat16 [256, 512, 512], P('shard', 'tensor'), as said below
- right_roots: bfloat16 [256, 512, 512], P('shard', 'tensor'), as said below
- row_moments: float32 [256, 512], P('shard'), may hold values from 0.003 to 0.05
- col_moments: float32 [256, 512], P('shard'), may hold values from 0.002 to 0.1
- owners: int32 [128], replicated, may hold values from 0 to 127, as said below
- emb_grads: bfloat16 [4, 4096, 4096], P('tensor', 'shard'), may hold values from -3 to 3
- emb_master: float32 [4096, 4096], P('shard', 'tensor'), may hold values from -0.75 to 0.75
- emb_mean: float32 [4096, 4096], P('shard', 'tensor'), may hold values from -0.75 to 0.75
- emb_var: float32 [4096, 4096], P('shard', 'tensor'), may hold values from 0.002 to 0.05
- gain_grads: bfloat16 [4, 2, 4096], P('tensor', None, 'shard'), may hold values from -3 to 3
- gain_master: float32 [2, 4096], P(None, ('shard', 'tensor')), may hold values from 0.5 to 1.5
- gain_mean: float32 [2, 4096], P(None, ('shard', 'tensor')), may hold values from -0.75 to 0.75
- gain_var: float32 [2, 4096], P(None, ('shard', 'tensor')), may hold values from 0.002 to 0.05
Outputs:
- wo_new: float32 [2, 8, 8, 512, 512], P(None, None, None, 'shard', 'tensor')
- wo_weights: bfloat16 [2, 8, 8, 512, 512], P(None, None, None, 'shard')
- left_new: float32 [256, 512, 512], P('shard', 'tensor')
- right_new: float32 [256, 512, 512], P('shard', 'tensor')
- row_new: float32 [256, 512], P('shard')
- col_new: float32 [256, 512], P('shard')
- emb_new: float32 [4096, 4096], P('shard', 'tensor')
- emb_mean_new: float32 [4096, 4096], P('shard', 'tensor')
- emb_var_new: float32 [4096, 4096], P('shard', 'tensor')
- emb_weights: bfloat16 [4096, 4096], P('shard')
- gain_new: float32 [2, 4096], P(None, ('shard', 'tensor'))
- gain_mean_new: float32 [2, 4096], P(None, ('shard', 'tensor'))
- gain_var_new: float32 [2, 4096], P(None, ('shard', 'tensor'))
- gain_weights: bfloat16 [2, 4096], P(None, 'shard')
Inputs may be any that keep to these rules, and one draw needn't show every extreme that they name: `owners`: each index of shard owns at most 2 of the 128 blocks, and some index owns exactly 2. `left_roots`: each slot's matrix is symmetric. `right_roots`: each slot's matrix is symmetric.
All inputs are finite; a program needn't handle non-finite values.
Results may differ from a plain program's by a relative error of at most 0.0052.
Values may be sent and summed in bfloat16 or wider, within the bound.
No kernel may reach another device: no remote copies, remote signals or barrier semaphores. Data moves between devices by JAX's collectives and lax.ppermute only.
A program may use at most 128 MiB of HBM per device.

v0:
```python
import jax
import jax.numpy as jnp
from jax import lax
from jax.sharding import PartitionSpec as P

beta_one = 0.9
beta_two = 0.95
bias_one = 1.0 - 0.9**10
bias_two = 1.0 - 0.95**10
adam_eps = 1e-08
learn_rate = 0.01
decay_rate = 0.1
graft_eps = 1e-06
factor_eps = 1e-08
highest = lax.Precision.HIGHEST


def slot_table(owners, slot_count, owner_count):
    block_ids = jnp.arange(owners.shape[0], dtype=jnp.int32)
    earlier = (owners[:, None] == owners[None, :]) & (block_ids[None, :] < block_ids[:, None])
    owner_rank = jnp.sum(earlier.astype(jnp.int32), axis=1)
    slot_of = owners * slot_count + owner_rank
    slot_ids = jnp.arange(slot_count * owner_count, dtype=jnp.int32)
    slot_hits = (slot_of[:, None] == slot_ids[None, :]).astype(jnp.int32)
    block_of = jnp.sum(slot_hits * block_ids[:, None], axis=0)
    slot_used = jnp.sum(slot_hits, axis=0)
    return (slot_of, block_of, slot_used)


def adamw_step(gradient, master, first_moment, second_moment):
    mean_new = beta_one * first_moment + (1.0 - beta_one) * gradient
    var_new = beta_two * second_moment + (1.0 - beta_two) * gradient * gradient
    adam_dir = mean_new / bias_one / (jnp.sqrt(var_new / bias_two) + adam_eps)
    master_new = master - learn_rate * (adam_dir + decay_rate * master)
    return (master_new, mean_new, var_new, master_new.astype(jnp.bfloat16))


def per_device(
    wo_grads,
    wo_master,
    left_stats,
    right_stats,
    left_roots,
    right_roots,
    row_moments,
    col_moments,
    owners,
    emb_grads,
    emb_master,
    emb_mean,
    emb_var,
    gain_grads,
    gain_master,
    gain_mean,
    gain_var,
):
    micro_count = lax.axis_size("tensor")
    owner_count = lax.axis_size("shard")
    tensor_pos = lax.axis_index("tensor")
    slot_count = left_stats.shape[0]
    quarter = left_stats.shape[1]
    slot_of, block_of, slot_used = slot_table(owners, slot_count, owner_count)
    left_full = lax.all_gather(left_roots, "tensor", axis=1, tiled=True)
    emb_terms = emb_grads[0].astype(jnp.float32)
    gain_terms = gain_grads[0].astype(jnp.float32)
    wo_terms = wo_grads[0].astype(jnp.float32)
    wo_sum, emb_sum, gain_sum = (
        lax.psum_scatter(wo_terms, "tensor", scatter_dimension=4, tiled=True),
        lax.psum_scatter(emb_terms, "tensor", scatter_dimension=1, tiled=True),
        lax.psum_scatter(gain_terms, "tensor", scatter_dimension=1, tiled=True),
    )
    wo_mean = wo_sum / micro_count
    rows_dev = wo_mean.shape[3]
    flattened = wo_mean.reshape(-1, rows_dev, quarter)
    taken = jnp.take(flattened, block_of, axis=0)
    outgoing = jnp.where(slot_used[:, None, None] > 0, taken, 0.0)
    outgoing = outgoing.reshape(owner_count, slot_count, rows_dev, quarter)
    own_cols = lax.all_to_all(outgoing, "shard", split_axis=0, concat_axis=2, tiled=True)[0]
    full_block = lax.all_gather(own_cols, "tensor", axis=2, tiled=True)
    own_rows = lax.dynamic_slice_in_dim(full_block, tensor_pos * quarter, quarter, 1)
    left_new = left_stats + jnp.einsum("sqj,sij->sqi", own_rows, full_block, precision=highest)
    right_new = right_stats + jnp.einsum("siq,sij->sqj", own_cols, full_block, precision=highest)
    squares = full_block * full_block
    row_new = beta_two * row_moments + (1.0 - beta_two) * jnp.mean(squares, axis=2)
    col_new = beta_two * col_moments + (1.0 - beta_two) * jnp.mean(squares, axis=1)
    row_level = jnp.mean(row_new, axis=1)
    col_part = lax.dynamic_slice_in_dim(col_new, tensor_pos * quarter, quarter, 1)
    second_est = row_new[:, :, None] * col_part[:, None, :] / row_level[:, None, None]
    adam_dir = own_cols / (jnp.sqrt(second_est) + factor_eps)
    adam_part = jnp.sum(adam_dir * adam_dir, axis=(1, 2))
    adam_total = lax.psum(adam_part, "tensor")
    right_half = jnp.einsum(
        "sij,sqj->siq",
        full_block.astype(jnp.bfloat16),
        right_roots,
        preferred_element_type=jnp.float32,
    ).astype(jnp.bfloat16)
    shampoo = jnp.einsum("sik,skq->siq", left_full, right_half, preferred_element_type=jnp.float32)
    shampoo_part = jnp.sum(shampoo * shampoo, axis=(1, 2))
    shampoo_total = lax.psum(shampoo_part, "tensor")
    graft_ratio = jnp.sqrt(adam_total) / (jnp.sqrt(shampoo_total) + graft_eps)
    update = shampoo * graft_ratio[:, None, None]
    returned = lax.all_to_all(update, "shard", split_axis=1, concat_axis=0, tiled=True)
    local_update = jnp.take(returned, slot_of, axis=0).reshape(wo_master.shape)
    wo_new = wo_master - learn_rate * (local_update + decay_rate * wo_master)
    emb_grad = emb_sum / micro_count
    gain_grad = gain_sum / micro_count
    emb_new, emb_mean_new, emb_var_new, emb_low = adamw_step(
        emb_grad, emb_master, emb_mean, emb_var
    )
    gain_new, gain_mean_new, gain_var_new, gain_low = adamw_step(
        gain_grad, gain_master, gain_mean, gain_var
    )
    wo_weights, emb_weights, gain_weights = (
        lax.all_gather(wo_new.astype(jnp.bfloat16), "tensor", axis=4, tiled=True),
        lax.all_gather(emb_low, "tensor", axis=1, tiled=True),
        lax.all_gather(gain_low, "tensor", axis=1, tiled=True),
    )
    return (
        wo_new,
        wo_weights,
        left_new,
        right_new,
        row_new,
        col_new,
        emb_new,
        emb_mean_new,
        emb_var_new,
        emb_weights,
        gain_new,
        gain_mean_new,
        gain_var_new,
        gain_weights,
    )


def solution(mesh):
    in_specs = (
        P("tensor", None, None, None, "shard", None),
        P(None, None, None, "shard", "tensor"),
        P("shard", "tensor", None),
        P("shard", "tensor", None),
        P("shard", "tensor", None),
        P("shard", "tensor", None),
        P("shard", None),
        P("shard", None),
        P(),
        P("tensor", "shard", None),
        P("shard", "tensor"),
        P("shard", "tensor"),
        P("shard", "tensor"),
        P("tensor", None, "shard"),
        P(None, ("shard", "tensor")),
        P(None, ("shard", "tensor")),
        P(None, ("shard", "tensor")),
    )
    out_specs = (
        P(None, None, None, "shard", "tensor"),
        P(None, None, None, "shard", None),
        P("shard", "tensor", None),
        P("shard", "tensor", None),
        P("shard", None),
        P("shard", None),
        P("shard", "tensor"),
        P("shard", "tensor"),
        P("shard", "tensor"),
        P("shard", None),
        P(None, ("shard", "tensor")),
        P(None, ("shard", "tensor")),
        P(None, ("shard", "tensor")),
        P(None, "shard"),
    )
    return jax.shard_map(
        per_device, mesh=mesh, in_specs=in_specs, out_specs=out_specs, check_vma=False
    )
```

profile of v0, /device:TPU:40, one launch (start us, length us, event | category | flops | bytes accessed | tf_op | source)
XLA Modules:
  0.0 324.4 jit_solution(10380883053698371560)
XLA Ops:
  7.2 0.0 copy-start
  7.2 0.0 reduce-scatter.8.cloned.1.call-start
  7.2 1.2 bitcast_convert_fusion
  8.5 26.2 %copy.74 = f32[2,8,8,4,512]{3,2,1,0,4:T(8,128)} copy(f32[2,8,8,4,512]{4,3,2,1,0:T(4,128)S(1)} %bitcast_convert_fusion) | data formatting | bytes 2097152
  34.7 29.3 %reshape.124 = f32[512,512]{1,0:T(8,128)} reshape(f32[512,2,8,8,4]{4,3,2,1,0:T(8,128)} %bitcast.45) | data formatting | bytes 2097152
  64.0 0.0 reduce-scatter.8.cloned.1.call-update
  64.1 0.0 all-gather.4.cloned.1.call-start
  64.1 0.2 convert_reduce_fusion.1
  64.3 0.5 compare_and_fusion.1
  64.8 0.1 convert_reduce_fusion
  64.9 0.4 copy-done.12
  65.3 0.1 reduce_sum.79
  65.5 0.2 gt.18
  65.7 33.9 %reduce-scatter.8.cloned.1.call-done = f32[128,512]{1,0:T(8,128)} async-done(((f32[512,512]{1,0:T(8,128)}), f32[128,512]{1,0:T(8,128)}) %reduce-scatter.8.cloned.1.call-update) | async-done | bytes 262160
  99.6 10.8 %reshape.125 = f32[128,2,8,8,4]{4,3,2,1,0:T(8,128)} reshape(f32[128,512]{1,0:T(8,128)} %reduce-scatter.8.cloned.1.call-done) | data formatting | bytes 524288
  110.5 6.6 %copy.75 = f32[2,8,8,4,128]{4,3,2,1,0:T(4,128)S(1)} copy(f32[2,8,8,4,128]{3,2,1,0,4:T(8,128)} %bitcast.46) | data formatting | bytes 524288
  117.1 0.1 broadcast_multiply_fusion
  117.2 1.0 gather_fusion
  118.2 0.5 select_select_fusion
  118.7 0.0 copy-start.5
  118.8 0.2 copy.61
  118.9 0.0 copy-start.17
  119.0 48.5 %all_to_all.33 = f32[128,2,4,128]{3,1,2,0:T(2,128)S(1)} all-to-all(f32[128,2,4,128]{3,1,2,0:T(2,128)S(1)} %copy.61), channel_id=1, replica_groups=mesh['shard'=128,'tensor'=4] {'shard'}, dimensions={0} | all-to-all | bytes 1048576 | tf_op jit(solution)/shard_map/all_to_all | solution.py:78
  167.5 0.9 copy.62
  168.4 0.0 all-gather.4.cloned.1.call-update
  168.4 0.0 all-gather.6.cloned.1.call-start
  168.5 0.7 all-gather.6.cloned.1.call-update
  169.2 0.0 reduce-scatter.6.cloned.1.call-start
  169.2 0.8 bitcast_convert_fusion.1
  170.0 0.0 reduce-scatter.6.cloned.1.call-update
  170.1 0.6 bitcast_convert_fusion.2
  170.6 30.6 %all-gather.4.cloned.1.call-done = f32[2,512,512]{2,1,0:T(8,128)} async-done(((f32[2,512,128]{2,1,0:T(8,128)}), f32[2,512,512]{2,1,0:T(8,128)}) %all-gather.4.cloned.1.call-update) | async-done | bytes 2097168 | tf_op jit(solution)/shard_map/all_gather | solution.py:79
  201.2 2.0 multiply_reduce_fusion
  203.3 0.1 fusion.8
  203.4 0.0 copy-start.9
  203.4 0.9 copy.73
  204.3 0.5 broadcast_multiply_fusion.1
  204.8 31.3 %all-gather.6.cloned.1.call-done = bf16[2,512,512]{2,1,0:T(8,128)(2,1)} async-done(((bf16[2,128,512]{2,1,0:T(8,128)(2,1)}), bf16[2,512,512]{2,1,0:T(8,128)(2,1)}) %all-gather.6.cloned.1.call-update) | async-done | bytes 1048592 | tf_op jit(solution)/shard_map/all_gather | solution.py:63
  236.1 2.2 multiply_reduce_fusion.2
  238.3 0.0 copy-start.13
  238.3 2.3 multiply_reduce_fusion.3
  240.6 10.0 %all-reduce.1 = (f32[2]{0:T(128)S(1)}, f32[2]{0:T(128)S(1)}, f32[2,32]{1,0:T(2,128)}) all-reduce(f32[2]{0:T(128)S(1)} %get-tuple-element.35, f32[2]{0:T(128)S(1)} %multiply_reduce_fusion.3, f32[2,32]{1,0:T(2,128)} %bitcast_convert_fusion.2), channel_id=1, replica_groups=mesh['shard'=128,'tensor'=4] {'tensor'}, use_global_device_ids=true, to_apply=%region_10.11 | all-reduce | flops 68 | bytes 544 | tf_op jit(solution)/shard_map/psum | solution.py:100
  250.6 0.0 copy-start.15
  250.6 0.1 multiply_bitcast_fusion
  250.7 1.0 copy.65
  251.7 16.6 %all-to-all-start.1 = ((f32[2,512,128]{2,0,1:T(2,128)}), f32[2,512,128]{2,0,1:T(2,128)S(1)}, u32[]{:S(2)}, u32[]{:S(2)}) async-start(f32[2,512,128]{2,0,1:T(2,128)} %copy.65), calls=%async_computation.1 | async-start | bytes 1048576 | tf_op jit(solution)/shard_map/all_to_all | solution.py:103
  268.3 0.7 broadcast_in_dim.48
  269.1 1.3 dynamic-slice
  271.0 0.0 copy-start.2
  271.0 0.0 reduce-scatter.6.cloned.1.call-done
  271.1 1.9 fusion.6
  273.0 13.1 %all_gather.18 = bf16[32,4096]{1,0:T(8,128)(2,1)} all-gather(bf16[32,1024]{1,0:T(8,128)(2,1)S(1)} %get-tuple-element.25), channel_id=1, replica_groups=mesh['shard'=128,'tensor'=4] {'tensor'}, dimensions={1}, use_global_device_ids=true | all-gather | bytes 327680 | tf_op jit(solution)/shard_map/all_gather | solution.py:116
  286.1 1.4 convert_bitcast_fusion
  287.4 7.3 %all-gather = bf16[4,8,2]{1,2,0:T(2,128)(2,1)S(1)} all-gather(bf16[1,8,2]{1,2,0:T(2,128)(2,1)S(1)} %get-tuple-element.21), channel_id=1, replica_groups=mesh['shard'=128,'tensor'=4] {'tensor'}, dimensions={0}, use_global_device_ids=true | all-gather | bytes 160 | tf_op jit(solution)/shard_map/all_gather | solution.py:117
  294.8 0.6 reshape.123
  295.4 4.1 %convolution_add_fusion.1 = f32[2,128,512]{2,1,0:T(8,128)} fusion(f32[2,128,512]{2,1,0:T(8,128)} %param.19, f32[2,512,512]{2,1,0:T(8,128)S(1)} %copy-done.1, s32[]{:T(128)S(6)} %select_n.46), kind=kOutput, calls=%fused_computation.5 | convolution fusion | flops 805437440 | bytes 3670020 | tf_op jit(solution)/shard_map/sqj,sij->sqi/dot_general | solution.py:81
  299.5 2.2 convolution_add_fusion
  301.7 0.4 copy.67
  302.1 0.3 copy.68
  302.5 0.7 gather_fusion.1
  303.3 0.9 fusion.7
  304.2 12.2 %all_gather.17 = bf16[2,8,8,4,512]{4,3,2,1,0:T(4,128)(2,1)S(1)} all-gather(bf16[2,8,8,4,128]{4,3,2,1,0:T(4,128)(2,1)S(1)} %get-tuple-element.29), channel_id=1, replica_groups=mesh['shard'=128,'tensor'=4] {'tensor'}, dimensions={4}, use_global_device_ids=true | all-gather | bytes 655360 | tf_op jit(solution)/shard_map/all_gather | solution.py:115
  316.4 0.8 copy.80
  317.2 0.7 copy.81
  (40 shorter events, 0.2 us)
Async XLA Ops:
  7.2 229.0 %copy-start = (bf16[2,128,512]{2,1,0:T(8,128)(2,1)S(1)}, bf16[2,128,512]{2,1,0:T(8,128)(2,1)}, u32[]{:S(2)}) copy-start(bf16[2,128,512]{2,1,0:T(8,128)(2,1)} %param.22) | copy-start | bytes 786436
  7.2 92.5 %reduce-scatter.8.cloned.1.call-start = ((), (), s32[]{:S(2)}) async-start(), calls=%async_computation.7 | async-start | bytes 1310720
  34.7 29.4 %copy-start.16 = (s32[128]{0:T(128)S(1)}, s32[128]{0:T(128)}, u32[]{:S(2)}) copy-start(s32[128]{0:T(128)} %param.25) | copy-start | bytes 1540
  64.1 137.2 %all-gather.4.cloned.1.call-start = ((), (), s32[]{:S(2)}) async-start(), calls=%async_computation.4 | async-start | bytes 2621440 | tf_op jit(solution)/shard_map/all_gather | solution.py:79
  64.8 0.5 copy-start.12
  118.7 50.5 %copy-start.5 = (bf16[1,32,4096]{2,1,0:T(8,128)(2,1)S(1)}, bf16[1,32,4096]{2,1,0:T(8,128)(2,1)}, u32[]{:S(2)}) copy-start(bf16[1,32,4096]{2,1,0:T(8,128)(2,1)} %param.26) | copy-start | bytes 786436
  118.9 51.1 %copy-start.17 = (bf16[1,2,32]{2,1,0:T(2,128)(2,1)S(1)}, bf16[1,2,32]{2,1,0:T(2,128)(2,1)}, u32[]{:S(2)}) copy-start(bf16[1,2,32]{2,1,0:T(2,128)(2,1)} %param.30) | copy-start | bytes 388
  168.4 34.9 %copy-start.10 = (f32[2,512]{1,0:T(2,128)S(1)}, f32[2,512]{1,0:T(2,128)}, u32[]{:S(2)}) copy-start(f32[2,512]{1,0:T(2,128)} %param.23) | copy-start | bytes 12292
  168.4 34.9 %copy-start.11 = (f32[2,512]{1,0:T(2,128)S(1)}, f32[2,512]{1,0:T(2,128)}, u32[]{:S(2)}) copy-start(f32[2,512]{1,0:T(2,128)} %param.24) | copy-start | bytes 12292
  168.4 67.7 %all-gather.6.cloned.1.call-start = ((), (), s32[]{:S(2)}) async-start(), calls=%async_computation.5 | async-start | bytes 1310720 | tf_op jit(solution)/shard_map/all_gather | solution.py:63
  169.2 101.9 %reduce-scatter.6.cloned.1.call-start = ((), (), s32[]{:S(2)}) async-start(), calls=%async_computation.6 | async-start | bytes 655360 | tf_op jit(solution)/shard_map/reduce_scatter | solution.py:69
  201.2 34.9 %copy-start.1 = (f32[2,512,512]{2,1,0:T(8,128)S(1)}, f32[2,512,512]{2,1,0:T(8,128)}, u32[]{:S(2)}) copy-start(f32[2,512,512]{2,1,0:T(8,128)} %all-gather.4.cloned.1.call-done) | copy-start | bytes 6291460
  203.4 34.9 %copy-start.8 = (f32[2,512]{1,0:T(2,128)}, f32[2,512]{1,0:T(2,128)S(1)}, u32[]{:S(2)}) copy-start(f32[2,512]{1,0:T(2,128)S(1)} %get-tuple-element.56) | copy-start | bytes 12292
  203.4 34.9 %copy-start.9 = (f32[2,512]{1,0:T(2,128)}, f32[2,512]{1,0:T(2,128)S(1)}, u32[]{:S(2)}) copy-start(f32[2,512]{1,0:T(2,128)S(1)} %get-tuple-element.57) | copy-start | bytes 12292
  238.3 32.8 %copy-start.7 = (f32[32,1024]{1,0:T(8,128)S(1)}, f32[32,1024]{1,0:T(8,128)}, u32[]{:S(2)}) copy-start(f32[32,1024]{1,0:T(8,128)} %param.27) | copy-start | bytes 393220
  238.3 32.7 %copy-start.13 = (s32[128]{0:T(128)S(1)}, s32[128]{0:T(128)}, u32[]{:S(2)}) copy-start(s32[128]{0:T(128)} %copy-done.12) | copy-start | bytes 1540
  250.6 35.5 %copy-start.14 = (f32[2,8]{1,0:T(2,128)S(1)}, f32[2,8]{1,0:T(2,128)}, u32[]{:S(2)}) copy-start(f32[2,8]{1,0:T(2,128)} %param.31) | copy-start | bytes 196
  250.6 35.5 %copy-start.15 = (f32[2,8]{1,0:T(2,128)S(1)}, f32[2,8]{1,0:T(2,128)}, u32[]{:S(2)}) copy-start(f32[2,8]{1,0:T(2,128)} %param.32) | copy-start | bytes 196
  251.7 50.0 %all-to-all-start.1 = ((f32[2,512,128]{2,0,1:T(2,128)}), f32[2,512,128]{2,0,1:T(2,128)S(1)}, u32[]{:S(2)}, u32[]{:S(2)}) async-start(f32[2,512,128]{2,0,1:T(2,128)} %copy.65), calls=%async_computation.1 | async-start | bytes 1048576 | tf_op jit(solution)/shard_map/all_to_all | solution.py:103
  271.0 28.5 %copy-start.2 = (f32[1,2,128,4,128]{4,3,2,1,0:T(4,128)S(1)}, f32[1,2,128,4,128]{4,3,2,1,0:T(4,128)}, u32[]{:S(2)}) copy-start(f32[1,2,128,4,128]{4,3,2,1,0:T(4,128)} %copy.62) | copy-start | bytes 1572868
  295.4 4.1 %copy-start.4 = (f32[2,128,512]{2,1,0:T(8,128)S(1)}, f32[2,128,512]{2,1,0:T(8,128)}, u32[]{:S(2)}) copy-start(f32[2,128,512]{2,1,0:T(8,128)} %param.20) | copy-start | bytes 1572868
  301.7 1.6 copy-start.6
  302.1 15.1 %copy-start.3 = (bf16[32,4096]{1,0:T(8,128)(2,1)S(1)}, bf16[32,4096]{1,0:T(8,128)(2,1)}, u32[]{:S(2)}) copy-start(bf16[32,4096]{1,0:T(8,128)(2,1)} %all_gather.18) | copy-start | bytes 786436
Sparse Core Ops, SparseCore 0:
  64.2 35.4 reduce-scatter.7
  168.5 32.6 all-gather.3
  203.3 32.7 all-gather.5
  239.4 29.7 reduce-scatter.5
where the time goes:
time: 325 us; the launch traced here: 324 us
  waiting for transfers between devices  96.6 us (30%)
  blocking collectives  91.1 us (28%)
  local copies, waits for them, and re-layouts  83.5 us (26%)
  starting transfers between devices  16.8 us (5%)
  between operations  14.8 us (5%)
  other arithmetic  13.3 us (4%)
  matrix products  8.48 us (3%)
    unnamed x44, local copies, waits for them, and re-layouts  76.9 us
    all_to_all x1, blocking collectives, per_device(): lax.all_to_all(outgoing, 'shard', split_axis=0, concat_axis=2, tiled=True)  48.5 us
    unnamed x5, waiting for transfers between devices  34.7 us
    all_gather x1, waiting for transfers between devices, per_device(): left_full = lax.all_gather(left_roots, 'tensor', axis=1, tiled=True)  31.3 us
    all_gather x1, waiting for transfers between devices, per_device(): full_block = lax.all_gather(own_cols, 'tensor', axis=2, tiled=True)  30.6 us
    all_to_all x1, starting transfers between devices, per_device(): lax.all_to_all(update, 'shard', split_axis=1, concat_axis=0, tiled=True)  16.6 us
    all_gather x1, blocking collectives, per_device(): lax.all_gather(emb_low, 'tensor', axis=1, tiled=True)  13.1 us
    all_gather x1, blocking collectives, per_device(): lax.all_gather(wo_new.astype(jnp.bfloat16), 'tensor', axis=4, tiled=True)  12.2 us
  transfers between devices with their start and end apart: 5, of which 3 were waited for; matrix products, arithmetic and copies ran while one was open for 7% of the time, Pallas kernels for 0%

commit v1 on v0

--- a/solution.py
+++ b/solution.py
@@ -13,6 +13,20 @@
 graft_eps = 1e-06
 factor_eps = 1e-08
 highest = lax.Precision.HIGHEST
+
+
+def follow_the_goods(s0):
+    lanes = lax.axis_size("tensor")
+    high, side_arr = (s0, 0)
+    while 1 << side_arr < lanes:
+        last = lax.ppermute(
+            high,
+            axis_name="tensor",
+            perm=list(map(lambda src_i: (src_i, src_i ^ 1 << side_arr), range(lanes))),
+        )
+        high = high + last
+        side_arr = side_arr + 1
+    return high
 
 
 def slot_table(owners, slot_count, owner_count):
@@ -97,7 +111,7 @@
     ).astype(jnp.bfloat16)
     shampoo = jnp.einsum("sik,skq->siq", left_full, right_half, preferred_element_type=jnp.float32)
     shampoo_part = jnp.sum(shampoo * shampoo, axis=(1, 2))
-    shampoo_total = lax.psum(shampoo_part, "tensor")
+    shampoo_total = follow_the_goods(shampoo_part)
     graft_ratio = jnp.sqrt(adam_total) / (jnp.sqrt(shampoo_total) + graft_eps)
     update = shampoo * graft_ratio[:, None, None]
     returned = lax.all_to_all(update, "shard", split_axis=1, concat_axis=0, tiled=True)

time: 325 us -> 336 us (1.034)
  the two profiles are of different devices: /device:TPU:40 before, /device:TPU:34 now
where the time goes in v1:
time: 336 us; the launch traced here: 335 us
  waiting for transfers between devices  99.2 us (30%)
  blocking collectives  92.7 us (28%)
  local copies, waits for them, and re-layouts  82.4 us (25%)
  starting transfers between devices  23.2 us (7%)
  between operations  14.8 us (4%)
  other arithmetic  13.9 us (4%)
  matrix products  8.99 us (3%)
    unnamed x40, local copies, waits for them, and re-layouts  76.5 us
    all_to_all x1, blocking collectives, per_device(): lax.all_to_all(outgoing, 'shard', split_axis=0, concat_axis=2, tiled=True)  49.4 us
    unnamed x5, waiting for transfers between devices  33 us
    all_gather x1, waiting for transfers between devices, per_device(): full_block = lax.all_gather(own_cols, 'tensor', axis=2, tiled=True)  31.2 us
    all_gather x1, waiting for transfers between devices, per_device(): left_full = lax.all_gather(left_roots, 'tensor', axis=1, tiled=True)  30.8 us
    all_to_all x1, starting transfers between devices, per_device(): lax.all_to_all(update, 'shard', split_axis=1, concat_axis=0, tiled=True)  16.6 us
    all_gather x1, blocking collectives, per_device(): lax.all_gather(emb_low, 'tensor', axis=1, tiled=True)  12.1 us
    all_gather x1, blocking collectives, per_device(): lax.all_gather(wo_new.astype(jnp.bfloat16), 'tensor', axis=4, tiled=True)  12 us
  transfers between devices with their start and end apart: 7, of which 4 were waited for; matrix products, arithmetic and copies ran while one was open for 7% of the time, Pallas kernels for 0%

profile of v1, /device:TPU:34, one launch (start us, length us, event | category | flops | bytes accessed | tf_op | source)
XLA Modules:
  0.0 335.2 jit_solution(16844900734075884010)
XLA Ops:
  7.2 0.0 copy-start
  7.2 0.0 reduce-scatter.8.cloned.1.call-start
  7.2 1.2 bitcast_convert_fusion
  8.5 26.2 %copy.74 = f32[2,8,8,4,512]{3,2,1,0,4:T(8,128)} copy(f32[2,8,8,4,512]{4,3,2,1,0:T(4,128)S(1)} %bitcast_convert_fusion) | data formatting | bytes 2097152
  34.7 29.3 %reshape.124 = f32[512,512]{1,0:T(8,128)} reshape(f32[512,2,8,8,4]{4,3,2,1,0:T(8,128)} %bitcast.45) | data formatting | bytes 2097152
  64.0 0.0 reduce-scatter.8.cloned.1.call-update
  64.1 0.0 all-gather.4.cloned.1.call-start
  64.1 0.2 convert_reduce_fusion.1
  64.3 0.5 compare_and_fusion.1
  64.8 0.1 convert_reduce_fusion
  64.9 0.1 reduce_sum.79
  65.1 0.2 gt.18
  65.3 32.3 %reduce-scatter.8.cloned.1.call-done = f32[128,512]{1,0:T(8,128)} async-done(((f32[512,512]{1,0:T(8,128)}), f32[128,512]{1,0:T(8,128)}) %reduce-scatter.8.cloned.1.call-update) | async-done | bytes 262160
  97.6 10.8 %reshape.125 = f32[128,2,8,8,4]{4,3,2,1,0:T(8,128)} reshape(f32[128,512]{1,0:T(8,128)} %reduce-scatter.8.cloned.1.call-done) | data formatting | bytes 524288
  108.4 6.6 %copy.75 = f32[2,8,8,4,128]{4,3,2,1,0:T(4,128)S(1)} copy(f32[2,8,8,4,128]{3,2,1,0,4:T(8,128)} %bitcast.46) | data formatting | bytes 524288
  115.0 0.1 broadcast_multiply_fusion
  115.1 1.0 gather_fusion
  116.2 0.5 select_select_fusion
  116.7 0.0 copy-start.5
  116.7 0.2 copy.61
  116.9 49.4 %all_to_all.33 = f32[128,2,4,128]{3,1,2,0:T(2,128)S(1)} all-to-all(f32[128,2,4,128]{3,1,2,0:T(2,128)S(1)} %copy.61), channel_id=1, replica_groups=mesh['shard'=128,'tensor'=4] {'shard'}, dimensions={0} | all-to-all | bytes 1048576 | tf_op jit(solution)/shard_map/all_to_all | solution.py:92
  166.3 0.9 copy.62
  167.2 0.0 all-gather.4.cloned.1.call-update
  167.2 0.0 all-gather.6.cloned.1.call-start
  167.3 0.7 all-gather.6.cloned.1.call-update
  168.0 0.0 reduce-scatter.6.cloned.1.call-start
  168.0 0.8 bitcast_convert_fusion.1
  168.8 0.0 reduce-scatter.6.cloned.1.call-update
  168.9 0.6 bitcast_convert_fusion.2
  169.4 31.2 %all-gather.4.cloned.1.call-done = f32[2,512,512]{2,1,0:T(8,128)} async-done(((f32[2,512,128]{2,1,0:T(8,128)}), f32[2,512,512]{2,1,0:T(8,128)}) %all-gather.4.cloned.1.call-update) | async-done | bytes 2097168 | tf_op jit(solution)/shard_map/all_gather | solution.py:93
  200.7 2.0 multiply_reduce_fusion
  202.7 0.1 fusion.8
  202.9 0.0 copy-start.9
  202.9 0.9 copy.73
  203.7 0.5 broadcast_multiply_fusion.1
  204.2 30.8 %all-gather.6.cloned.1.call-done = bf16[2,512,512]{2,1,0:T(8,128)(2,1)} async-done(((bf16[2,128,512]{2,1,0:T(8,128)(2,1)}), bf16[2,512,512]{2,1,0:T(8,128)(2,1)}) %all-gather.6.cloned.1.call-update) | async-done | bytes 1048592 | tf_op jit(solution)/shard_map/all_gather | solution.py:77
  235.1 2.7 multiply_reduce_fusion.2
  237.8 2.3 multiply_reduce_fusion.3
  240.0 3.6 %collective-permute-start = (f32[2]{0:T(128)}, f32[2]{0:T(128)S(1)}, u32[]{:S(2)}, u32[]{:S(2)}) collective-permute-start(f32[2]{0:T(128)} %get-tuple-element.34), channel_id=1, source_target_pairs={{0,1},{1,0},{2,3},{3,2},{4,5},{5,4},{6,7},{7,6},{8,9},{9,8},{10,11... | collective-permute-start | bytes 32 | tf_op jit(solution)/shard_map/ppermute | solution.py:22
  243.6 8.7 %all-reduce.1 = (f32[2]{0:T(128)S(1)}, f32[2,32]{1,0:T(2,128)}) all-reduce(f32[2]{0:T(128)S(1)} %multiply_reduce_fusion.3, f32[2,32]{1,0:T(2,128)} %bitcast_convert_fusion.2), channel_id=1, replica_groups=mesh['shard'=128,'tensor'=4] {'tensor'}, use_global_device_ids=true, to_apply=%region_8.9 | all-reduce | flops 66 | bytes 528 | tf_op jit(solution)/shard_map/psum | solution.py:105
  252.4 0.7 add.121
  253.0 2.8 collective-permute-start.1
  255.8 4.2 %collective-permute-done.1 = f32[2]{0:T(128)S(1)} collective-permute-done((f32[2]{0:T(128)S(1)}, f32[2]{0:T(128)S(1)}, u32[]{:S(2)}, u32[]{:S(2)}) %collective-permute-start.1) | collective-permute-done | bytes 40 | tf_op jit(solution)/shard_map/ppermute | solution.py:22
  260.0 0.1 multiply_bitcast_fusion
  260.2 1.0 copy.65
  261.1 16.6 %all-to-all-start.1 = ((f32[2,512,128]{2,0,1:T(2,128)}), f32[2,512,128]{2,0,1:T(2,128)S(1)}, u32[]{:S(2)}, u32[]{:S(2)}) async-start(f32[2,512,128]{2,0,1:T(2,128)} %copy.65), calls=%async_computation.1 | async-start | bytes 1048576 | tf_op jit(solution)/shard_map/all_to_all | solution.py:117
  277.8 0.1 broadcast_in_dim.48
  277.9 1.3 dynamic-slice
  279.8 0.0 copy-start.2
  279.9 0.0 reduce-scatter.6.cloned.1.call-done
  279.9 1.9 fusion.6
  281.8 12.1 %all_gather.18 = bf16[32,4096]{1,0:T(8,128)(2,1)} all-gather(bf16[32,1024]{1,0:T(8,128)(2,1)S(1)} %get-tuple-element.24), channel_id=1, replica_groups=mesh['shard'=128,'tensor'=4] {'tensor'}, dimensions={1}, use_global_device_ids=true | all-gather | bytes 327680 | tf_op jit(solution)/shard_map/all_gather | solution.py:130
  293.9 1.4 convert_bitcast_fusion
  295.2 10.5 %all-gather = bf16[4,8,2]{1,2,0:T(2,128)(2,1)S(1)} all-gather(bf16[1,8,2]{1,2,0:T(2,128)(2,1)S(1)} %get-tuple-element.20), channel_id=1, replica_groups=mesh['shard'=128,'tensor'=4] {'tensor'}, dimensions={0}, use_global_device_ids=true | all-gather | bytes 160 | tf_op jit(solution)/shard_map/all_gather | solution.py:131
  305.7 0.6 reshape.123
  306.3 4.1 %convolution_add_fusion.1 = f32[2,128,512]{2,1,0:T(8,128)} fusion(f32[2,128,512]{2,1,0:T(8,128)} %param.19, f32[2,512,512]{2,1,0:T(8,128)S(1)} %copy-done.1, s32[]{:T(128)S(6)} %select_n.46), kind=kOutput, calls=%fused_computation.5 | convolution fusion | flops 805437440 | bytes 3670020 | tf_op jit(solution)/shard_map/sqj,sij->sqi/dot_general | solution.py:95
  310.5 2.2 convolution_add_fusion
  312.7 0.4 copy.67
  313.1 0.3 copy.68
  313.5 0.7 gather_fusion.1
  314.2 0.9 fusion.7
  315.2 12.0 %all_gather.17 = bf16[2,8,8,4,512]{4,3,2,1,0:T(4,128)(2,1)S(1)} all-gather(bf16[2,8,8,4,128]{4,3,2,1,0:T(4,128)(2,1)S(1)} %get-tuple-element.28), channel_id=1, replica_groups=mesh['shard'=128,'tensor'=4] {'tensor'}, dimensions={4}, use_global_device_ids=true | all-gather | bytes 655360 | tf_op jit(solution)/shard_map/all_gather | solution.py:129
  327.2 0.8 copy.80
  328.0 0.7 copy.81
  (41 shorter events, 0.2 us)
Async XLA Ops:
  7.2 227.9 %copy-start = (bf16[2,128,512]{2,1,0:T(8,128)(2,1)S(1)}, bf16[2,128,512]{2,1,0:T(8,128)(2,1)}, u32[]{:S(2)}) copy-start(bf16[2,128,512]{2,1,0:T(8,128)(2,1)} %param.22) | copy-start | bytes 786436
  7.2 90.4 %reduce-scatter.8.cloned.1.call-start = ((), (), s32[]{:S(2)}) async-start(), calls=%async_computation.7 | async-start | bytes 1310720
  34.7 29.4 %copy-start.14 = (s32[128]{0:T(128)S(1)}, s32[128]{0:T(128)}, u32[]{:S(2)}) copy-start(s32[128]{0:T(128)} %param.25) | copy-start | bytes 1540
  64.1 136.6 %all-gather.4.cloned.1.call-start = ((), (), s32[]{:S(2)}) async-start(), calls=%async_computation.4 | async-start | bytes 2621440 | tf_op jit(solution)/shard_map/all_gather | solution.py:93
  116.7 51.3 %copy-start.5 = (bf16[1,32,4096]{2,1,0:T(8,128)(2,1)S(1)}, bf16[1,32,4096]{2,1,0:T(8,128)(2,1)}, u32[]{:S(2)}) copy-start(bf16[1,32,4096]{2,1,0:T(8,128)(2,1)} %param.26) | copy-start | bytes 786436
  116.9 52.0 %copy-start.15 = (bf16[1,2,32]{2,1,0:T(2,128)(2,1)S(1)}, bf16[1,2,32]{2,1,0:T(2,128)(2,1)}, u32[]{:S(2)}) copy-start(bf16[1,2,32]{2,1,0:T(2,128)(2,1)} %param.30) | copy-start | bytes 388
  167.2 35.5 %copy-start.10 = (f32[2,512]{1,0:T(2,128)S(1)}, f32[2,512]{1,0:T(2,128)}, u32[]{:S(2)}) copy-start(f32[2,512]{1,0:T(2,128)} %param.23) | copy-start | bytes 12292
  167.2 35.5 %copy-start.11 = (f32[2,512]{1,0:T(2,128)S(1)}, f32[2,512]{1,0:T(2,128)}, u32[]{:S(2)}) copy-start(f32[2,512]{1,0:T(2,128)} %param.24) | copy-start | bytes 12292
  167.2 67.8 %all-gather.6.cloned.1.call-start = ((), (), s32[]{:S(2)}) async-start(), calls=%async_computation.5 | async-start | bytes 1310720 | tf_op jit(solution)/shard_map/all_gather | solution.py:77
  168.0 111.9 %reduce-scatter.6.cloned.1.call-start = ((), (), s32[]{:S(2)}) async-start(), calls=%async_computation.6 | async-start | bytes 655360 | tf_op jit(solution)/shard_map/reduce_scatter | solution.py:83
  200.7 34.4 %copy-start.1 = (f32[2,512,512]{2,1,0:T(8,128)S(1)}, f32[2,512,512]{2,1,0:T(8,128)}, u32[]{:S(2)}) copy-start(f32[2,512,512]{2,1,0:T(8,128)} %all-gather.4.cloned.1.call-done) | copy-start | bytes 6291460
  202.9 34.9 %copy-start.8 = (f32[2,512]{1,0:T(2,128)}, f32[2,512]{1,0:T(2,128)S(1)}, u32[]{:S(2)}) copy-start(f32[2,512]{1,0:T(2,128)S(1)} %get-tuple-element.55) | copy-start | bytes 12292
  202.9 34.9 %copy-start.9 = (f32[2,512]{1,0:T(2,128)}, f32[2,512]{1,0:T(2,128)S(1)}, u32[]{:S(2)}) copy-start(f32[2,512]{1,0:T(2,128)S(1)} %get-tuple-element.56) | copy-start | bytes 12292
  237.8 42.1 %copy-start.7 = (f32[32,1024]{1,0:T(8,128)S(1)}, f32[32,1024]{1,0:T(8,128)}, u32[]{:S(2)}) copy-start(f32[32,1024]{1,0:T(8,128)} %param.27) | copy-start | bytes 393220
  237.8 40.0 %copy-start.12 = (pred[128]{0:T(512)(128)(4,1)S(1)}, pred[128]{0:T(512)(128)(4,1)}, u32[]{:S(2)}) copy-start(pred[128]{0:T(512)(128)(4,1)} %get-tuple-element.30) | copy-start | bytes 388
  240.0 12.4 %collective-permute-start = (f32[2]{0:T(128)}, f32[2]{0:T(128)S(1)}, u32[]{:S(2)}, u32[]{:S(2)}) collective-permute-start(f32[2]{0:T(128)} %get-tuple-element.34), channel_id=1, source_target_pairs={{0,1},{1,0},{2,3},{3,2},{4,5},{5,4},{6,7},{7,6},{8,9},{9,8},{10,11... | collective-permute-start | bytes 32 | tf_op jit(solution)/shard_map/ppermute | solution.py:22
  253.0 7.0 %collective-permute-start.1 = (f32[2]{0:T(128)S(1)}, f32[2]{0:T(128)S(1)}, u32[]{:S(2)}, u32[]{:S(2)}) collective-permute-start(f32[2]{0:T(128)S(1)} %add.121), channel_id=1, source_target_pairs={{0,2},{1,3},{2,0},{3,1},{4,6},{5,7},{6,4},{7,5},{8,10},{9,11},{10,... | collective-permute-start | bytes 32 | tf_op jit(solution)/shard_map/ppermute | solution.py:22
  260.0 33.9 %copy-start.13 = (f32[2,8]{1,0:T(2,128)S(1)}, f32[2,8]{1,0:T(2,128)}, u32[]{:S(2)}) copy-start(f32[2,8]{1,0:T(2,128)} %param.31) | copy-start | bytes 196
  261.1 51.5 %all-to-all-start.1 = ((f32[2,512,128]{2,0,1:T(2,128)}), f32[2,512,128]{2,0,1:T(2,128)S(1)}, u32[]{:S(2)}, u32[]{:S(2)}) async-start(f32[2,512,128]{2,0,1:T(2,128)} %copy.65), calls=%async_computation.1 | async-start | bytes 1048576 | tf_op jit(solution)/shard_map/all_to_all | solution.py:117
  279.8 30.6 %copy-start.2 = (f32[1,2,128,4,128]{4,3,2,1,0:T(4,128)S(1)}, f32[1,2,128,4,128]{4,3,2,1,0:T(4,128)}, u32[]{:S(2)}) copy-start(f32[1,2,128,4,128]{4,3,2,1,0:T(4,128)} %copy.62) | copy-start | bytes 1572868
  306.3 4.1 %copy-start.4 = (f32[2,128,512]{2,1,0:T(8,128)S(1)}, f32[2,128,512]{2,1,0:T(8,128)}, u32[]{:S(2)}) copy-start(f32[2,128,512]{2,1,0:T(8,128)} %param.20) | copy-start | bytes 1572868
  312.7 1.6 copy-start.6
  313.1 14.8 %copy-start.3 = (bf16[32,4096]{1,0:T(8,128)(2,1)S(1)}, bf16[32,4096]{1,0:T(8,128)(2,1)}, u32[]{:S(2)}) copy-start(bf16[32,4096]{1,0:T(8,128)(2,1)} %all_gather.18) | copy-start | bytes 786436
Sparse Core Ops, SparseCore 0:
  64.2 33.3 reduce-scatter.7
  167.3 33.2 all-gather.3
  202.8 32.2 all-gather.5
  238.3 28.8 reduce-scatter.5
